TPU v7x, 32 devices: a whole 2x2x4 slice. The times are simulated.
32 devices in a mesh: wide: 8 (over y, x, core), blk: 4 (over z).
Axes of the slice: x: 2, y: 2, z: 4, core: 2. Of those that a mesh axis runs over, the one named last changes fastest.
Arguments:
- left_points: float32 [4096], P(('wide', 'blk')), may hold values from -1 to 1, as said below
- left_ports: int32 [4096], P(('wide', 'blk')), may hold values from 0 to 63
- left_values: bfloat16 [4096, 64], P(('wide', 'blk')), may hold values from -6 to 6
- right_points: float32 [2048], P('blk'), may hold values from -1 to 1
- right_ports: int32 [2048], P('blk'), may hold values from 0 to 63
- right_values: bfloat16 [2048, 64], P('blk'), may hold values from -6 to 6
- sketch_block: int32 [2048], P('blk'), may hold values from 0 to 63, as said below
- sketch_weight: bfloat16 [2048], P('blk'), may hold values from -1 to 1
Outputs:
- basis: float32 [4096, 64], P(('wide', 'blk'))
- projected: float32 [64, 64], replicated
Inputs may be any that keep to these rules, and one draw needn't show every extreme that they name: `left_points`: no left point lies closer than 0.6 / 2048 to any right point. `sketch_block`: in every aligned run of 64 right samples each sketch column appears exactly once.
All inputs are finite; a program needn't handle non-finite values.
Results may differ from a plain program's by a relative error of at most 0.0019.
Values sent between devices are 32-bit elements; how exact they have to be, the bound alone decides.
No kernel may reach another device: no remote copies, remote signals or barrier semaphores. Data moves between devices by JAX's collectives and lax.ppermute only.
A program may use at most 64 MiB of HBM per device.

v0:
```python
import jax
import jax.numpy as jnp
from jax import lax
from jax.sharding import PartitionSpec as P

K = 64


def cholesky_lower(gram):
    order = gram.shape[0]
    index_ids = jnp.arange(order, dtype=jnp.int32)

    def column_step(j, lower):
        row_j = lax.dynamic_slice_in_dim(lower, j, 1, 0)[0]
        column = lax.dynamic_slice_in_dim(gram, j, 1, 1)[:, 0] - jnp.dot(
            lower, row_j, precision=lax.Precision.HIGHEST
        )
        pivot = jnp.sqrt(lax.dynamic_slice_in_dim(column, j, 1, 0)[0])
        fresh = jnp.where(
            index_ids > j,
            column / pivot,
            jnp.where(index_ids == j, pivot, jnp.zeros((), gram.dtype)),
        )
        marker = (index_ids == j).astype(gram.dtype)
        return lower + fresh[:, None] * marker[None, :]

    return lax.fori_loop(0, order, column_step, jnp.zeros_like(gram))


def solve_lower(lower, rhs):
    order = lower.shape[0]
    index_ids = jnp.arange(order, dtype=jnp.int32)

    def row_step(j, result):
        row_j = lax.dynamic_slice_in_dim(lower, j, 1, 0)[0]
        pivot = lax.dynamic_slice_in_dim(row_j, j, 1, 0)[0]
        target = lax.dynamic_slice_in_dim(rhs, j, 1, 0)[0]
        value = (target - jnp.dot(row_j, result, precision=lax.Precision.HIGHEST)) / pivot
        marker = (index_ids == j).astype(rhs.dtype)
        return result + marker[:, None] * value[None, :]

    return lax.fori_loop(0, order, row_step, jnp.zeros_like(rhs))


def solve_upper(upper, rhs):
    order = upper.shape[0]
    index_ids = jnp.arange(order, dtype=jnp.int32)

    def row_step(step, result):
        j = order - 1 - step
        row_j = lax.dynamic_slice_in_dim(upper, j, 1, 0)[0]
        pivot = lax.dynamic_slice_in_dim(row_j, j, 1, 0)[0]
        target = lax.dynamic_slice_in_dim(rhs, j, 1, 0)[0]
        value = (target - jnp.dot(row_j, result, precision=lax.Precision.HIGHEST)) / pivot
        marker = (index_ids == j).astype(rhs.dtype)
        return result + marker[:, None] * value[None, :]

    return lax.fori_loop(0, order, row_step, jnp.zeros_like(rhs))


def tile_sketch(left_freq, left_onehot, left_values, points, ports, values_block, columns, weights):
    amount = points.shape[0]
    block_count = amount // amount
    port_ids = jnp.arange(left_values.shape[1], dtype=jnp.int32)
    column_ids = jnp.arange(K, dtype=jnp.int32)

    def absorb(carry, items):
        freq, port_block, value_rows, column_block, weight_block = items
        onehot_right = (port_ids[:, None] == port_block[None, :]).astype(jnp.float32)
        num_v = jnp.dot(
            left_values,
            onehot_right,
            precision=lax.Precision.HIGHEST,
            preferred_element_type=jnp.float32,
        )
        num_w = lax.dot_general(
            left_onehot,
            value_rows,
            (((1,), (1,)), ((), ())),
            precision=lax.Precision.HIGHEST,
            preferred_element_type=jnp.float32,
        )
        inverse = 1.0 / (left_freq[:, None] - freq[None, :])
        loewner = (num_v - num_w) * inverse
        shifted = (left_freq[:, None] * num_v - freq[None, :] * num_w) * inverse
        omega = jnp.where(
            column_block[:, None] == column_ids[None, :],
            weight_block[:, None],
            jnp.zeros((), jnp.float32),
        )
        sketch_part = jnp.dot(
            loewner, omega, precision=lax.Precision.HIGHEST, preferred_element_type=jnp.float32
        )
        shift_part = jnp.dot(
            shifted, omega, precision=lax.Precision.HIGHEST, preferred_element_type=jnp.float32
        )
        return ((carry[0] + sketch_part, carry[1] + shift_part), None)

    row_count = left_values.shape[0]
    start_carry = (jnp.zeros((row_count, K), jnp.float32), jnp.zeros((row_count, K), jnp.float32))
    items = (
        points.reshape(block_count, amount),
        ports.reshape(block_count, amount),
        values_block.reshape(block_count, amount, values_block.shape[1]),
        columns.reshape(block_count, amount),
        weights.reshape(block_count, amount),
    )
    result, _ = lax.scan(absorb, start_carry, items)
    return result


def left_setup(points, ports, width):
    port_ids = jnp.arange(width, dtype=jnp.int32)
    onehot_left = (ports[:, None] == port_ids[None, :]).astype(jnp.float32)
    return (points, onehot_left)


def per_device(
    left_points,
    left_ports,
    left_values,
    right_points,
    right_ports,
    right_values,
    sketch_block,
    sketch_weight,
):
    row_count = left_points.shape[0]
    width = left_values.shape[1]
    left_wide = left_values.astype(jnp.float32)
    group_points, group_ports, group_values = (
        lax.all_gather(left_points, "blk", axis=0, tiled=True),
        lax.all_gather(left_ports, "blk", axis=0, tiled=True),
        lax.all_gather(left_wide, "blk", axis=0, tiled=True),
    )
    right_wide = right_values.astype(jnp.float32)
    weight_wide = sketch_weight.astype(jnp.float32)
    left_freq, left_onehot = left_setup(group_points, group_ports, width)
    sketch_part, shift_part = tile_sketch(
        left_freq,
        left_onehot,
        group_values,
        right_points,
        right_ports,
        right_wide,
        sketch_block,
        weight_wide,
    )
    stacked = lax.psum_scatter(
        jnp.concatenate([sketch_part, shift_part], axis=1), "blk", scatter_dimension=0, tiled=True
    )
    sketch = stacked[:, :K]
    shifted_sketch = stacked[:, K:]
    row_total = row_count * lax.axis_size("wide") * lax.axis_size("blk")
    gram_local = jnp.dot(sketch.T, sketch, precision=lax.Precision.HIGHEST)
    gram = lax.psum(gram_local, ("wide", "blk")) / row_total
    lower = cholesky_lower(gram)
    basis_t = solve_lower(lower, sketch.T)
    projection_local = jnp.dot(basis_t, shifted_sketch, precision=lax.Precision.HIGHEST)
    coefficient = lax.psum(projection_local, ("wide", "blk")) / row_total
    projected = solve_upper(lower.T, coefficient)
    return (basis_t.T, projected)


def solution(mesh):
    placed = (
        P(("wide", "blk")),
        P(("wide", "blk")),
        P(("wide", "blk"), None),
        P("blk"),
        P("blk"),
        P("blk", None),
        P("blk"),
        P("blk"),
    )
    return jax.shard_map(
        per_device,
        mesh=mesh,
        in_specs=placed,
        out_specs=(P(("wide", "blk"), None), P()),
        check_vma=False,
    )
```

profile of v0, /device:TPU:0, one launch (start us, length us, event | category | flops | bytes accessed | tf_op | source)
XLA Modules:
  0.0 438.6 jit_solution(5190188491721261414)
XLA Ops:
  7.9 15.1 %all_gather.9 = f32[512,64]{0,1:T(8,128)S(1)} all-gather(f32[128,64]{0,1:T(8,128)S(1)} %convert_element_type.55), channel_id=1, replica_groups=mesh['wide'=8,'blk'=4] {'blk'}, dimensions={0}, use_global_device_ids=true | all-gather | bytes 163840 | tf_op jit(solution)/shard_map/all_gather | solution.py:134
  23.7 11.2 %all-gather = s32[4,1,128]{2,1,0:T(1,128)S(1)} all-gather(s32[1,1,128]{2,1,0:T(1,128)S(1)} %bitcast.82), channel_id=1, replica_groups=mesh['wide'=8,'blk'=4] {'blk'}, dimensions={0}, use_global_device_ids=true | all-gather | bytes 2560 | tf_op jit(solution)/shard_map/all_gather | solution.py:133
  35.6 7.7 %all-gather.1 = f32[4,1,128]{2,1,0:T(1,128)S(1)} all-gather(f32[1,1,128]{2,1,0:T(1,128)S(1)} %bitcast.83), channel_id=1, replica_groups=mesh['wide'=8,'blk'=4] {'blk'}, dimensions={0}, use_global_device_ids=true | all-gather | bytes 2560 | tf_op jit(solution)/shard_map/all_gather | solution.py:132
  45.3 1.1 fusion.28
  46.4 1.0 fusion.33
  48.1 19.8 %reduce-scatter.2.cloned.1.call-done = f32[128,128]{0,1:T(8,128)} async-done(((f32[512,128]{0,1:T(8,128)}), f32[128,128]{0,1:T(8,128)}) %reduce-scatter.2.cloned.1.call-update) | async-done | bytes 65552 | tf_op jit(solution)/shard_map/reduce_scatter | solution.py:149
  67.9 1.0 fusion.55
  68.9 38.6 %psum.14 = f32[64,64]{1,0:T(8,128)S(1)} all-reduce(f32[64,64]{1,0:T(8,128)S(1)} %fusion.55), channel_id=1, replica_groups=mesh['wide'=8,'blk'=4] {'wide','blk'}, use_global_device_ids=true, to_apply=%region_1.2 | all-reduce | flops 4096 | bytes 32768 | tf_op jit(solution)/shard_map/psum | solution.py:156
  107.7 94.5 %while.57 = (s32[]{:T(128)}, f32[64,64]{1,0:T(8,128)S(1)}, f32[64,64]{0,1:T(8,128)S(1)}, s32[]{:T(128)}, s32[]{:T(128)}) while((s32[]{:T(128)}, f32[64,64]{1,0:T(8,128)S(1)}, f32[64,64]{0,1:T(8,128)S(1)}, s32[]{:T(128)}, s32[]{:T(128)}) %tuple.124), condition=%wide.region_3.4_spmd.clone.clone, body=%wide.region_2.3_spmd.clone.clone.sunk | while | flops 66051 | bytes 101992 | solution.py:27
  202.2 93.7 %while.55 = (s32[]{:T(128)}, f32[64,128]{1,0:T(8,128)S(1)}, f32[64,128]{1,0:T(8,128)S(1)}, f32[64,64]{1,0:T(8,128)S(1)}, s32[]{:T(128)}, /*index=5*/s32[]{:T(128)}, s32[]{:T(128)}) while((s32[]{:T(128)}, f32[64,128]{1,0:T(8,128)S(1)}, f32[64,128]{1,0:T(8,128)S(1)}, f32[64,64]{1,0:T(8,128)S(1)}, s32[]{:T(128)}, ...), condition=%wide.region_5.6_spmd.clone, body=%wide.region_4.5_spmd.clone.sunk | while | flops 131460 | bytes 102520 | solution.py:42
  202.8 0.8 fusion.76
  204.3 0.8 fusion.76
  205.7 0.8 fusion.76
  207.2 0.8 fusion.76
  208.7 0.8 fusion.76
  210.1 0.8 fusion.76
  211.6 0.8 fusion.76
  213.1 0.8 fusion.76
  214.5 0.8 fusion.76
  216.0 0.8 fusion.76
  217.5 0.8 fusion.76
  218.9 0.8 fusion.76
  220.4 0.8 fusion.76
  223.3 0.8 fusion.76
  226.2 0.8 fusion.76
  245.3 0.8 fusion.76
  248.2 0.8 fusion.76
  251.1 0.8 fusion.76
  254.1 0.8 fusion.76
  273.1 0.8 fusion.76
  276.0 0.8 fusion.76
  279.0 0.8 fusion.76
  281.9 0.8 fusion.76
  296.6 40.8 %psum.15 = f32[64,64]{1,0:T(8,128)S(1)} all-reduce(f32[64,64]{1,0:T(8,128)S(1)} %fusion.53), channel_id=1, replica_groups=mesh['wide'=8,'blk'=4] {'wide','blk'}, use_global_device_ids=true, to_apply=%region_6.7 | all-reduce | flops 4096 | bytes 32768 | tf_op jit(solution)/shard_map/psum | solution.py:160
  337.5 93.7 %while.56 = (s32[]{:T(128)}, f32[64,64]{1,0:T(8,128)S(1)}, f32[64,64]{1,0:T(8,128)S(1)}, f32[64,64]{1,0:T(8,128)S(1)}, s32[]{:T(128)}, /*index=5*/s32[]{:T(128)}, s32[]{:T(128)}, s32[]{:T(128)}) while((s32[]{:T(128)}, f32[64,64]{1,0:T(8,128)S(1)}, f32[64,64]{1,0:T(8,128)S(1)}, f32[64,64]{1,0:T(8,128)S(1)}, s32[]{:T(128)}, ...), condition=%wide.region_8.9_spmd.clone, body=%wide.region_7.8_spmd.clone.sunk | while | flops 65800 | bytes 69297 | solution.py:58
  342.5 0.8 fusion.79
  348.3 0.8 fusion.79
  355.6 0.8 fusion.79
  363.0 0.8 fusion.79
  370.3 0.8 fusion.79
  376.1 0.8 fusion.79
  383.5 0.8 fusion.79
  390.8 0.8 fusion.79
  398.1 0.8 fusion.79
  403.9 0.8 fusion.79
  411.3 0.8 fusion.79
  418.6 0.8 fusion.79
  425.9 0.8 fusion.79
  (896 shorter events, 219.6 us)
Async XLA Ops:
  7.2 37.4 %copy-start = (bf16[512,64]{0,1:T(8,128)(2,1)S(1)}, bf16[512,64]{0,1:T(8,128)(2,1)}, u32[]{:S(2)}) copy-start(bf16[512,64]{0,1:T(8,128)(2,1)} %param.19) | copy-start | bytes 196612
  7.2 60.7 %reduce-scatter.2.cloned.1.call-start = ((), (), s32[]{:S(2)}) async-start(), calls=%async_computation.1 | async-start | bytes 327680 | tf_op jit(solution)/shard_map/reduce_scatter | solution.py:149
  23.0 0.7 copy-start.6
  34.9 0.7 copy-start.7
  35.6 7.7 %copy-start.5 = (bf16[512]{0:T(512)(128)(2,1)S(1)}, bf16[512]{0:T(512)(128)(2,1)}, u32[]{:S(2)}) copy-start(bf16[512]{0:T(512)(128)(2,1)} %param.21) | copy-start | bytes 3076
  43.3 0.7 copy-start.4
  44.6 0.7 copy-start.8
  44.6 0.7 copy-start.9
  107.7 94.5 %copy-start.3 = (f32[128,128]{0,1:T(8,128)S(1)}, f32[128,128]{0,1:T(8,128)}, u32[]{:S(2)}) copy-start(f32[128,128]{0,1:T(8,128)} %reduce-scatter.2.cloned.1.call-done) | copy-start | bytes 196612
  295.9 0.6 copy-start.1
  431.2 0.6 copy-start.2
Sparse Core Ops, SparseCore 0:
  48.2 19.6 reduce-scatter.1
where the time goes:
time: 441 us; the launch traced here: 439 us
  local copies, waits for them, and re-layouts  119 us (27%)
  matrix products  114 us (26%)
  blocking collectives  113 us (26%)
  loops' own time  40.3 us (9%)
  waiting for transfers between devices  19.8 us (4%)
  other arithmetic  18.2 us (4%)
  between operations  14.2 us (3%)
    dot_general x128, matrix products, row_step(): jnp.dot(row_j, result, precision=lax.Precision.HIGHEST)  100 us
    dynamic_slice x128, local copies, waits for them, and re-layouts, row_step(): pivot = lax.dynamic_slice_in_dim(row_j, j, 1, 0)[0]  76.2 us
    psum x1, blocking collectives, per_device(): coefficient = lax.psum(projection_local, ('wide', 'blk')) / row_total  40.8 us
    another operation x1, loops' own time, cholesky_lower(): return lax.fori_loop(0, order, column_step, jnp.zeros_like(gram))  40 us
    dynamic_slice x64, local copies, waits for them, and re-layouts, column_step(): pivot = jnp.sqrt(lax.dynamic_slice_in_dim(column, j, 1, 0)[0])  39.2 us
    psum x1, blocking collectives, per_device(): gram = lax.psum(gram_local, ('wide', 'blk')) / row_total  38.6 us
    reduce_scatter x1, waiting for transfers between devices, per_device(): lax.psum_scatter(jnp.concatenate([sketch_part, shift_part], axis=1), 'blk...  19.8 us
    all_gather x1, blocking collectives, per_device(): lax.all_gather(left_wide, 'blk', axis=0, tiled=True)  15.1 us
  transfers between devices with their start and end apart: 1, of which 1 were waited for; matrix products, arithmetic and copies ran while one was open for 0% of the time, Pallas kernels for 0%

commit v1 on v0

--- a/solution.py
+++ b/solution.py
@@ -157,7 +157,7 @@
     lower = cholesky_lower(gram)
     basis_t = solve_lower(lower, sketch.T)
     projection_local = jnp.dot(basis_t, shifted_sketch, precision=lax.Precision.HIGHEST)
-    coefficient = lax.psum(projection_local, ("wide", "blk")) / row_total
+    coefficient = lax.psum(lax.psum(projection_local, "wide"), "blk") / row_total
     projected = solve_upper(lower.T, coefficient)
     return (basis_t.T, projected)
 

time: 441 us -> 446 us (1.011)
    psum x1 -> x2, blocking collectives: 40.8 us -> 41.1 us  [the longest x1 23.1 us: per_device(): lax.psum(projection_local, 'wide')]
where the time goes in v1:
time: 446 us; the launch traced here: 444 us
  local copies, waits for them, and re-layouts  120 us (27%)
  blocking collectives  114 us (26%)
  matrix products  114 us (26%)
  loops' own time  44.1 us (10%)
  waiting for transfers between devices  19.8 us (4%)
  other arithmetic  18.2 us (4%)
  between operations  14.2 us (3%)
    dot_general x128, matrix products, row_step(): jnp.dot(row_j, result, precision=lax.Precision.HIGHEST)  100 us
    dynamic_slice x128, local copies, waits for them, and re-layouts, row_step(): pivot = lax.dynamic_slice_in_dim(row_j, j, 1, 0)[0]  76.2 us
    another operation x1, loops' own time, cholesky_lower(): return lax.fori_loop(0, order, column_step, jnp.zeros_like(gram))  43.8 us
    dynamic_slice x64, local copies, waits for them, and re-layouts, column_step(): pivot = jnp.sqrt(lax.dynamic_slice_in_dim(column, j, 1, 0)[0])  40.2 us
    psum x1, blocking collectives, per_device(): gram = lax.psum(gram_local, ('wide', 'blk')) / row_total  38.6 us
    psum x1, blocking collectives, per_device(): lax.psum(projection_local, 'wide')  23.1 us
    reduce_scatter x1, waiting for transfers between devices, per_device(): lax.psum_scatter(jnp.concatenate([sketch_part, shift_part], axis=1), 'blk...  19.8 us
    psum x1, blocking collectives, per_device(): lax.psum(lax.psum(projection_local, 'wide'), 'blk') / row_total  17.9 us
  transfers between devices with their start and end apart: 1, of which 1 were waited for; matrix products, arithmetic and copies ran while one was open for 0% of the time, Pallas kernels for 0%

profile of v1, /device:TPU:0, one launch (start us, length us, event | category | flops | bytes accessed | tf_op | source)
XLA Modules:
  0.0 443.6 jit_solution(6099787579286923594)
XLA Ops:
  7.9 15.1 %all_gather.9 = f32[512,64]{0,1:T(8,128)S(1)} all-gather(f32[128,64]{0,1:T(8,128)S(1)} %convert_element_type.55), channel_id=1, replica_groups=mesh['wide'=8,'blk'=4] {'blk'}, dimensions={0}, use_global_device_ids=true | all-gather | bytes 163840 | tf_op jit(solution)/shard_map/all_gather | solution.py:134
  23.7 11.2 %all-gather = s32[4,1,128]{2,1,0:T(1,128)S(1)} all-gather(s32[1,1,128]{2,1,0:T(1,128)S(1)} %bitcast.82), channel_id=1, replica_groups=mesh['wide'=8,'blk'=4] {'blk'}, dimensions={0}, use_global_device_ids=true | all-gather | bytes 2560 | tf_op jit(solution)/shard_map/all_gather | solution.py:133
  35.6 7.7 %all-gather.1 = f32[4,1,128]{2,1,0:T(1,128)S(1)} all-gather(f32[1,1,128]{2,1,0:T(1,128)S(1)} %bitcast.83), channel_id=1, replica_groups=mesh['wide'=8,'blk'=4] {'blk'}, dimensions={0}, use_global_device_ids=true | all-gather | bytes 2560 | tf_op jit(solution)/shard_map/all_gather | solution.py:132
  45.3 1.1 fusion.28
  46.4 1.0 fusion.33
  48.1 19.8 %reduce-scatter.2.cloned.1.call-done = f32[128,128]{0,1:T(8,128)} async-done(((f32[512,128]{0,1:T(8,128)}), f32[128,128]{0,1:T(8,128)}) %reduce-scatter.2.cloned.1.call-update) | async-done | bytes 65552 | tf_op jit(solution)/shard_map/reduce_scatter | solution.py:149
  67.9 1.0 fusion.55
  68.9 38.6 %psum.21 = f32[64,64]{1,0:T(8,128)S(1)} all-reduce(f32[64,64]{1,0:T(8,128)S(1)} %fusion.55), channel_id=1, replica_groups=mesh['wide'=8,'blk'=4] {'wide','blk'}, use_global_device_ids=true, to_apply=%region_1.2 | all-reduce | flops 4096 | bytes 32768 | tf_op jit(solution)/shard_map/psum | solution.py:156
  107.7 99.3 %while.57 = (s32[]{:T(128)}, f32[64,64]{1,0:T(8,128)S(1)}, f32[64,64]{0,1:T(8,128)S(1)}, s32[]{:T(128)}, s32[]{:T(128)}) while((s32[]{:T(128)}, f32[64,64]{1,0:T(8,128)S(1)}, f32[64,64]{0,1:T(8,128)S(1)}, s32[]{:T(128)}, s32[]{:T(128)}) %tuple.124), condition=%wide.region_3.4_spmd.clone.clone, body=%wide.region_2.3_spmd.clone.clone.sunk | while | flops 66051 | bytes 101992 | solution.py:27
  207.0 93.7 %while.55 = (s32[]{:T(128)}, f32[64,128]{1,0:T(8,128)S(1)}, f32[64,128]{1,0:T(8,128)S(1)}, f32[64,64]{1,0:T(8,128)S(1)}, s32[]{:T(128)}, /*index=5*/s32[]{:T(128)}, s32[]{:T(128)}) while((s32[]{:T(128)}, f32[64,128]{1,0:T(8,128)S(1)}, f32[64,128]{1,0:T(8,128)S(1)}, f32[64,64]{1,0:T(8,128)S(1)}, s32[]{:T(128)}, ...), condition=%wide.region_5.6_spmd.clone, body=%wide.region_4.5_spmd.clone.sunk | while | flops 131460 | bytes 102520 | solution.py:42
  207.6 0.8 fusion.76
  209.1 0.8 fusion.76
  210.5 0.8 fusion.76
  212.0 0.8 fusion.76
  213.5 0.8 fusion.76
  214.9 0.8 fusion.76
  216.4 0.8 fusion.76
  217.8 0.8 fusion.76
  219.3 0.8 fusion.76
  220.8 0.8 fusion.76
  222.2 0.8 fusion.76
  223.7 0.8 fusion.76
  226.6 0.8 fusion.76
  229.6 0.8 fusion.76
  248.6 0.8 fusion.76
  251.5 0.8 fusion.76
  254.5 0.8 fusion.76
  257.4 0.8 fusion.76
  276.4 0.8 fusion.76
  279.3 0.8 fusion.76
  282.3 0.8 fusion.76
  285.2 0.8 fusion.76
  301.3 23.1 %psum.22 = f32[64,64]{1,0:T(8,128)S(1)} all-reduce(f32[64,64]{1,0:T(8,128)S(1)} %fusion.53), channel_id=1, replica_groups=mesh['wide'=8,'blk'=4] {'wide'}, use_global_device_ids=true, to_apply=%region_6.7 | all-reduce | flops 4096 | bytes 32768 | tf_op jit(solution)/shard_map/psum | solution.py:160
  324.5 17.9 %psum.23 = f32[64,64]{1,0:T(8,128)S(1)} all-reduce(f32[64,64]{1,0:T(8,128)S(1)} %psum.22), channel_id=1, replica_groups=mesh['wide'=8,'blk'=4] {'blk'}, use_global_device_ids=true, to_apply=%region_7.8 | all-reduce | flops 4096 | bytes 32768 | tf_op jit(solution)/shard_map/psum | solution.py:160
  342.5 93.7 %while.56 = (s32[]{:T(128)}, f32[64,64]{1,0:T(8,128)S(1)}, f32[64,64]{1,0:T(8,128)S(1)}, f32[64,64]{1,0:T(8,128)S(1)}, s32[]{:T(128)}, /*index=5*/s32[]{:T(128)}, s32[]{:T(128)}, s32[]{:T(128)}) while((s32[]{:T(128)}, f32[64,64]{1,0:T(8,128)S(1)}, f32[64,64]{1,0:T(8,128)S(1)}, f32[64,64]{1,0:T(8,128)S(1)}, s32[]{:T(128)}, ...), condition=%wide.region_9.10_spmd.clone, body=%wide.region_8.9_spmd.clone.sunk | while | flops 65800 | bytes 69297 | solution.py:58
  346.0 0.8 fusion.79
  353.3 0.8 fusion.79
  360.7 0.8 fusion.79
  368.0 0.8 fusion.79
  373.8 0.8 fusion.79
  381.1 0.8 fusion.79
  388.5 0.8 fusion.79
  395.8 0.8 fusion.79
  401.6 0.8 fusion.79
  409.0 0.8 fusion.79
  416.3 0.8 fusion.79
  423.6 0.8 fusion.79
  429.4 0.8 fusion.79
  (897 shorter events, 221.4 us)
Async XLA Ops:
  7.2 37.4 %copy-start = (bf16[512,64]{0,1:T(8,128)(2,1)S(1)}, bf16[512,64]{0,1:T(8,128)(2,1)}, u32[]{:S(2)}) copy-start(bf16[512,64]{0,1:T(8,128)(2,1)} %param.19) | copy-start | bytes 196612
  7.2 60.7 %reduce-scatter.2.cloned.1.call-start = ((), (), s32[]{:S(2)}) async-start(), calls=%async_computation.1 | async-start | bytes 327680 | tf_op jit(solution)/shard_map/reduce_scatter | solution.py:149
  23.0 0.7 copy-start.6
  34.9 0.7 copy-start.7
  35.6 7.7 %copy-start.5 = (bf16[512]{0:T(512)(128)(2,1)S(1)}, bf16[512]{0:T(512)(128)(2,1)}, u32[]{:S(2)}) copy-start(bf16[512]{0:T(512)(128)(2,1)} %param.21) | copy-start | bytes 3076
  43.3 0.7 copy-start.4
  44.6 0.7 copy-start.8
  44.6 0.7 copy-start.9
  107.7 99.3 %copy-start.3 = (f32[128,128]{0,1:T(8,128)S(1)}, f32[128,128]{0,1:T(8,128)}, u32[]{:S(2)}) copy-start(f32[128,128]{0,1:T(8,128)} %reduce-scatter.2.cloned.1.call-done) | copy-start | bytes 196612
  300.7 0.6 copy-start.1
  436.2 0.6 copy-start.2
Sparse Core Ops, SparseCore 0:
  48.2 19.6 reduce-scatter.1
